TPU v7x, 512 devices: a whole 4x8x8 slice. The times are simulated.
512 devices in a mesh: dp: 32 (over x, y), table: 16 (over z, core).
Axes of the slice: x: 4, y: 8, z: 8, core: 2. Of those that a mesh axis runs over, the one named last changes fastest.
Arguments:
- table: bfloat16 [12288, 512], P('table'), may hold values from -6 to 6
- history_shard: int32 [512, 256, 1], P(('dp', 'table')), may hold values from 0 to 15; in each aligned block of 256 rows (0 to 255, 256 to 511, ..., all dimensions but the last counted through in order) at most 32 rows name the same one
- history_row: int32 [512, 256], P(('dp', 'table')), may hold values from 0 to 767
- lengths: int32 [512], P(('dp', 'table')), may hold values from 1 to 256, 98304 in all
- w_in: bfloat16 [512, 2048], replicated, may hold values from -0.25 to 0.25
- w_out: bfloat16 [512, 512], replicated, may hold values from -0.25 to 0.25
- cotangent: bfloat16 [512, 256, 512], P(('dp', 'table')), may hold values from -6 to 6
Outputs:
- table_grad: float32 [12288, 512], P('table')
- dense_grad: bfloat16 [512, 512], replicated
Inputs may be any that keep to these rules, and one draw needn't show every extreme that they name: `history_shard`: among the 256 history slots of one device's samples, at most 32 name one table shard, and that bound is met by some shard in some device's slots. `lengths`: some sample has the full length 256.
All inputs are finite; a program needn't handle non-finite values. No bound on the sum of `lengths` on one device may be relied on, other than what follows from the above.
Results may differ from a plain program's by a relative error of at most 0.017.
Values may be sent and summed in bfloat16 or wider, within the bound.
A program may use at most 64 MiB of HBM per device.

v0:
```python
import math
import jax
import jax.numpy as jnp
from jax import lax
from jax.sharding import PartitionSpec as P

HEADS = 4


def layer_norm(values):
    average = jnp.mean(values, axis=-1, keepdims=True)
    centred = values - average
    variance = jnp.mean(centred * centred, axis=-1, keepdims=True)
    return centred * lax.rsqrt(variance + 1e-06)


def hstu_layer(embedded, w_in, w_out, lengths):
    samples_here, seq_span, model_width = embedded.shape
    head_dim = model_width // HEADS
    normed = layer_norm(embedded.astype(jnp.float32)).astype(jnp.bfloat16)
    projected = jax.nn.silu(
        jnp.dot(
            normed.reshape(samples_here * seq_span, model_width),
            w_in,
            preferred_element_type=jnp.float32,
        )
    )
    gate_part = projected[:, :model_width]
    shaped = (samples_here, seq_span, HEADS, head_dim)
    values = projected[:, model_width : 2 * model_width].astype(jnp.bfloat16).reshape(shaped)
    queries = projected[:, 2 * model_width : 3 * model_width].astype(jnp.bfloat16).reshape(shaped)
    keys = projected[:, 3 * model_width :].astype(jnp.bfloat16).reshape(shaped)
    scores = jnp.einsum(
        "blhd,bmhd->bhlm", queries.astype(jnp.float32), keys.astype(jnp.float32)
    ) * head_dim ** (-0.5)
    positions = jnp.arange(seq_span)
    live_keys = (positions[None, None, :] <= positions[None, :, None]) & (
        positions[None, None, :] < lengths[:, None, None]
    )
    weights = (
        jnp.where(live_keys[:, None], jax.nn.silu(scores), 0.0)
        / lengths.astype(jnp.float32)[:, None, None, None]
    )
    weights = weights.astype(jnp.bfloat16)
    attended = jnp.einsum(
        "bhlm,bmhd->blhd", weights.astype(jnp.float32), values.astype(jnp.float32)
    ).reshape(samples_here * seq_span, model_width)
    mixed = (layer_norm(attended) * gate_part).astype(jnp.bfloat16)
    output = jnp.dot(mixed, w_out, preferred_element_type=jnp.float32) + embedded.reshape(
        -1, model_width
    ).astype(jnp.float32)
    return (output, mixed)


def per_device(table, history_shard, history_row, lengths, w_in, w_out, cotangent):
    shard_rows, model_width = table.shape
    samples_here, seq_span = history_row.shape
    groups = lax.axis_size("table")
    slot_count = samples_here * seq_span
    capacity = 2 * slot_count // groups
    owners = history_shard[:, :, 0].reshape(-1)
    local_rows = history_row.reshape(-1)
    owner_hits = (owners[:, None] == jnp.arange(groups)[None, :]).astype(jnp.int32)
    slot_rank = jnp.sum((jnp.cumsum(owner_hits, axis=0) - owner_hits) * owner_hits, axis=1)
    position = owners * capacity + slot_rank
    requested = (
        jnp.zeros((groups * capacity,), jnp.int32)
        .at[position]
        .set(local_rows)
        .reshape(groups, capacity)
    )
    incoming = lax.all_to_all(requested, "table", split_axis=0, concat_axis=0, tiled=True).reshape(
        -1
    )
    global_rows = owners * shard_rows + local_rows
    piece = lax.all_gather(table, "table", axis=0, tiled=True)
    inside = (global_rows >= 0) & (global_rows < piece.shape[0])
    taken = piece[jnp.clip(global_rows, 0, piece.shape[0] - 1)].astype(jnp.float32)
    embedded = jnp.where(inside[:, None], taken, 0.0).astype(jnp.bfloat16)
    embedded = embedded.reshape(samples_here, seq_span, model_width)
    output, pullback, mixed = jax.vjp(
        lambda rows_in: hstu_layer(rows_in, w_in, w_out, lengths), embedded, has_aux=True
    )
    row_live = jnp.arange(seq_span)[None, :] < lengths[:, None]
    grad_seed = jnp.where(row_live[:, :, None], cotangent, jnp.zeros_like(cotangent))
    flat_seed = grad_seed.reshape(-1, model_width)
    (row_grad,) = pullback(flat_seed.astype(jnp.float32))
    dense_part = jnp.dot(mixed.T, flat_seed, preferred_element_type=jnp.float32)
    outgoing = (
        jnp.zeros((groups * capacity, model_width), jnp.bfloat16)
        .at[position]
        .set(row_grad.reshape(-1, model_width))
    )
    arrived = lax.all_to_all(
        outgoing.reshape(groups, capacity, model_width),
        "table",
        split_axis=0,
        concat_axis=0,
        tiled=True,
    )
    local_grad = (
        jnp.zeros((shard_rows, model_width), jnp.float32)
        .at[incoming]
        .add(arrived.reshape(-1, model_width).astype(jnp.float32))
    )
    total_slots = slot_count * lax.axis_size("dp") * groups
    grad_scale = 1.0 / math.sqrt(total_slots)
    table_grad = lax.psum(local_grad, "dp")
    dense_total = lax.psum(dense_part, ("dp", "table"))
    dense_grad = (dense_total * grad_scale).astype(jnp.bfloat16)
    return (table_grad, dense_grad)


def solution(mesh):
    in_specs = (
        P("table", None),
        P(("dp", "table"), None, None),
        P(("dp", "table"), None),
        P(("dp", "table")),
        P(),
        P(),
        P(("dp", "table"), None, None),
    )
    out_specs = (P("table", None), P())
    return jax.shard_map(
        per_device, mesh=mesh, in_specs=in_specs, out_specs=out_specs, check_vma=False
    )
```

profile of v0, /device:TPU:64, one launch (start us, length us, event | category | flops | bytes accessed | tf_op | source)
XLA Modules:
  0.0 582.9 jit_solution(10138484838293075610)
XLA Ops:
  7.2 0.0 copy-start
  7.2 0.0 all-gather.2.cloned.1.call-start
  7.2 0.7 all-gather.2.cloned.1.call-update
  7.9 0.7 fusion.64
  8.6 0.6 reduce-window.6
  9.2 0.2 slice_reduce_fusion
  9.4 0.8 fusion.63
  10.2 0.7 compare_select_fusion.1
  10.9 1.6 scatter_custom_fusion
  12.4 0.7 all_to_all.9
  13.1 10.0 %all-to-all-start = ((s32[16,1,32]{2,1,0:T(1,128)}), s32[16,1,32]{2,1,0:T(1,128)S(1)}, u32[]{:S(2)}, u32[]{:S(2)}) async-start(s32[16,1,32]{2,1,0:T(1,128)} %all_to_all.9), calls=%async_computation | async-start | bytes 16384 | tf_op jit(solution)/shard_map/all_to_all | solution.py:72
  23.8 0.7 compare_and_fusion
  24.5 66.3 %all-gather.2.cloned.1.call-done = bf16[12288,512]{1,0:T(8,128)(2,1)} async-done(((bf16[768,512]{1,0:T(8,128)(2,1)}), bf16[12288,512]{1,0:T(8,128)(2,1)}) %all-gather.2.cloned.1.call-update) | async-done | bytes 12582928 | tf_op jit(solution)/shard_map/all_gather | solution.py:76
  90.8 7.4 %gather_fusion = bf16[256,512]{1,0:T(8,128)(2,1)S(1)} fusion(bf16[12288,512]{1,0:T(8,128)(2,1)} %all-gather.2.cloned.1.call-done, s32[1024]{0:T(1024)S(1)} %pad_clamp_fusion), kind=kCustom, calls=%fused_computation | custom fusion | bytes 525312 | tf_op jit(solution)/shard_map/gather | solution.py:78
  98.2 0.2 convert_reduce_fusion
  98.4 0.2 fusion.38
  98.6 0.0 copy-done
  98.7 2.8 fusion.76
  101.5 0.8 slice_bitcast_fusion
  102.2 0.1 copy.40
  102.4 0.0 copy-start.4
  102.4 0.1 copy.41
  102.5 0.0 copy-start.6
  102.5 0.0 copy-start.8
  102.5 1.6 divide_convert_fusion
  104.1 0.0 copy-done.4
  104.1 0.0 copy-done.6
  104.1 0.0 copy-done.8
  104.1 0.3 fusion.78
  104.5 0.1 fusion.40
  104.6 0.3 copy-done.2
  104.9 0.2 copy.35
  105.1 1.7 multiply_reduce_fusion.1
  106.9 2.1 fusion.75
  108.9 0.1 broadcast_add_fusion
  109.0 0.1 copy.36
  109.2 0.0 copy-start.5
  109.2 2.0 fusion.26
  111.3 0.2 fusion.80
  111.5 0.0 copy-done.7
  111.5 1.0 fusion.79
  112.5 0.9 fusion.81
  113.5 0.1 copy.37
  113.6 1.8 copy.38
  115.4 1.8 copy.39
  117.2 3.4 multiply_reduce_fusion
  120.6 1.0 fusion.74
  121.6 2.9 scatter_custom_fusion.1
  124.5 0.0 all-to-all-done
  124.5 6.9 %all-to-all-start.1 = ((bf16[16,32,512]{2,1,0:T(8,128)(2,1)}), bf16[16,32,512]{2,1,0:T(8,128)(2,1)}, u32[]{:S(2)}, u32[]{:S(2)}) async-start(bf16[16,32,512]{2,1,0:T(8,128)(2,1)} %bitcast.120), calls=%async_computation.1 | async-start | bytes 1048576 | tf_op jit(solution)/shard_map/all_to_all | solution.py:94
  131.4 0.2 all-reduce.9.cloned.1.call-start
  131.6 2.5 fusion.45
  134.1 0.0 all-reduce.9.cloned.1.call-update
  134.1 0.0 all-reduce.7.cloned.1.call-start
  134.2 0.5 broadcast.379
  134.7 0.7 reduce.15
  135.4 0.1 reshape.502
  135.4 10.4 %all-to-all-done.1 = bf16[16,32,512]{2,1,0:T(8,128)(2,1)} async-done(((bf16[16,32,512]{2,1,0:T(8,128)(2,1)}), bf16[16,32,512]{2,1,0:T(8,128)(2,1)}, u32[]{:S(2)}, u32[]{:S(2)}) %all-to-all-start.1) | async-done | bytes 524320 | tf_op jit(solution)/shard_map/all_to_all | solution.py:94
  145.8 5.5 scatter_custom_fusion.2
  151.3 0.0 all-reduce.7.cloned.1.call-update
  151.3 258.6 %all-reduce.9.cloned.1.call-done = f32[512,512]{1,0:T(8,128)} async-done(((f32[512,512]{1,0:T(8,128)}), f32[512,512]{1,0:T(8,128)}) %all-reduce.9.cloned.1.call-update) | async-done | bytes 1048592 | tf_op jit(solution)/shard_map/psum | solution.py:109
  409.9 2.1 multiply_convert_fusion
  412.0 161.6 %all-reduce.7.cloned.1.call-done = f32[768,512]{1,0:T(8,128)} async-done(((f32[768,512]{1,0:T(8,128)}), f32[768,512]{1,0:T(8,128)}) %all-reduce.7.cloned.1.call-update) | async-done | bytes 1572880 | tf_op jit(solution)/shard_map/psum | solution.py:108
  573.7 2.7 copy.58
  (20 shorter events, 0.2 us)
Async XLA Ops:
  7.2 91.5 %copy-start = (bf16[512,2048]{1,0:T(8,128)(2,1)S(1)}, bf16[512,2048]{1,0:T(8,128)(2,1)}, u32[]{:S(2)}) copy-start(bf16[512,2048]{1,0:T(8,128)(2,1)} %param.11) | copy-start | bytes 6291460
  7.2 83.6 %all-gather.2.cloned.1.call-start = ((), (), s32[]{:S(2)}) async-start(), calls=%async_computation.2 | async-start | bytes 13369344 | tf_op jit(solution)/shard_map/all_gather | solution.py:76
  13.1 111.4 %all-to-all-start = ((s32[16,1,32]{2,1,0:T(1,128)}), s32[16,1,32]{2,1,0:T(1,128)S(1)}, u32[]{:S(2)}, u32[]{:S(2)}) async-start(s32[16,1,32]{2,1,0:T(1,128)} %all_to_all.9), calls=%async_computation | async-start | bytes 16384 | tf_op jit(solution)/shard_map/all_to_all | solution.py:72
  102.4 1.8 copy-start.4
  102.5 1.6 copy-start.6
  102.5 1.6 copy-start.8
  104.1 0.8 copy-start.2
  109.2 2.1 copy-start.5
  109.2 2.3 copy-start.7
  111.2 1.3 copy-start.3
  117.2 4.4 copy-start.1
  124.5 21.3 %all-to-all-start.1 = ((bf16[16,32,512]{2,1,0:T(8,128)(2,1)}), bf16[16,32,512]{2,1,0:T(8,128)(2,1)}, u32[]{:S(2)}, u32[]{:S(2)}) async-start(bf16[16,32,512]{2,1,0:T(8,128)(2,1)} %bitcast.120), calls=%async_computation.1 | async-start | bytes 1048576 | tf_op jit(solution)/shard_map/all_to_all | solution.py:94
  131.4 278.5 %all-reduce.9.cloned.1.call-start = ((), (), s32[]{:S(2)}) async-start(), calls=%async_computation.4 | async-start | bytes 2097152 | tf_op jit(solution)/shard_map/psum | solution.py:109
  134.1 439.6 %all-reduce.7.cloned.1.call-start = ((), (), s32[]{:S(2)}) async-start(), calls=%async_computation.3 | async-start | bytes 3145728 | tf_op jit(solution)/shard_map/psum | solution.py:108
Sparse Core Ops, SparseCore 0:
  10.1 80.5 all-gather.1
  137.3 272.5 all-reduce.8
  414.3 159.3 all-reduce.6
where the time goes:
time: 584 us; the launch traced here: 583 us
  waiting for transfers between devices  498 us (85%)
  local copies, waits for them, and re-layouts  18.5 us (3%)
  other arithmetic  18.5 us (3%)
  starting transfers between devices  17.1 us (3%)
  matrix products  16.5 us (3%)
  between operations  14.6 us (2%)
    psum x1, waiting for transfers between devices, per_device(): dense_total = lax.psum(dense_part, ('dp', 'table'))  259 us
    psum x1, waiting for transfers between devices, per_device(): table_grad = lax.psum(local_grad, 'dp')  162 us
    all_gather x1, waiting for transfers between devices, per_device(): piece = lax.all_gather(table, 'table', axis=0, tiled=True)  66.3 us
  transfers between devices with their start and end apart: 5, of which 4 were waited for; matrix products, arithmetic and copies ran while one was open for 9% of the time, Pallas kernels for 0%

commit v1 on v0

--- a/solution.py
+++ b/solution.py
@@ -105,7 +105,13 @@
     )
     total_slots = slot_count * lax.axis_size("dp") * groups
     grad_scale = 1.0 / math.sqrt(total_slots)
-    table_grad = lax.psum(local_grad, "dp")
+    size = lax.axis_size("dp")
+    table_grad, far = (local_grad, 1)
+    while far < size:
+        table_grad = table_grad + lax.ppermute(
+            table_grad, "dp", [(i, i ^ far) for i in range(size)]
+        )
+        far = 2 * far
     dense_total = lax.psum(dense_part, ("dp", "table"))
     dense_grad = (dense_total * grad_scale).astype(jnp.bfloat16)
     return (table_grad, dense_grad)

time: 584 us -> 672 us (1.15)
  the two profiles are of different devices: /device:TPU:64 before, /device:TPU:24 now
where the time goes in v1:
time: 672 us; the launch traced here: 671 us
  waiting for transfers between devices  565 us (84%)
  starting transfers between devices  32.7 us (5%)
  other arithmetic  25.7 us (4%)
  matrix products  16.5 us (2%)
  local copies, waits for them, and re-layouts  15.8 us (2%)
  between operations  15 us (2%)
    psum x1, waiting for transfers between devices, per_device(): dense_total = lax.psum(dense_part, ('dp', 'table'))  269 us
    ppermute x5, waiting for transfers between devices, per_device(): lax.ppermute(table_grad, 'dp', [(i, i ^ far) for i in range(size)])  212 us
    all_gather x1, waiting for transfers between devices, per_device(): piece = lax.all_gather(table, 'table', axis=0, tiled=True)  68.7 us
    ppermute x5, starting transfers between devices, per_device(): lax.ppermute(table_grad, 'dp', [(i, i ^ far) for i in range(size)])  17.8 us
    all_to_all x1, waiting for transfers between devices, per_device(): lax.all_to_all(outgoing.reshape(groups, capacity, model_width), 'table',...  14.6 us
  transfers between devices with their start and end apart: 9, of which 7 were waited for; matrix products, arithmetic and copies ran while one was open for 7% of the time, Pallas kernels for 0%

profile of v1, /device:TPU:24, one launch (start us, length us, event | category | flops | bytes accessed | tf_op | source)
XLA Modules:
  0.0 670.9 jit_solution(5140011026267119332)
XLA Ops:
  7.2 0.0 copy-start
  7.2 0.0 all-gather.2.cloned.1.call-start
  7.2 0.7 all-gather.2.cloned.1.call-update
  7.9 0.7 fusion.64
  8.6 0.6 reduce-window.6
  9.2 0.2 slice_reduce_fusion
  9.4 0.8 fusion.63
  10.2 0.7 compare_select_fusion.1
  10.9 1.6 scatter_custom_fusion
  12.4 0.7 all_to_all.9
  13.1 10.4 %all-to-all-start = ((s32[16,1,32]{2,1,0:T(1,128)}), s32[16,1,32]{2,1,0:T(1,128)S(1)}, u32[]{:S(2)}, u32[]{:S(2)}) async-start(s32[16,1,32]{2,1,0:T(1,128)} %all_to_all.9), calls=%async_computation | async-start | bytes 16384 | tf_op jit(solution)/shard_map/all_to_all | solution.py:72
  24.2 0.7 compare_and_fusion
  25.0 68.7 %all-gather.2.cloned.1.call-done = bf16[12288,512]{1,0:T(8,128)(2,1)} async-done(((bf16[768,512]{1,0:T(8,128)(2,1)}), bf16[12288,512]{1,0:T(8,128)(2,1)}) %all-gather.2.cloned.1.call-update) | async-done | bytes 12582928 | tf_op jit(solution)/shard_map/all_gather | solution.py:76
  93.6 7.4 %gather_fusion = bf16[256,512]{1,0:T(8,128)(2,1)S(1)} fusion(bf16[12288,512]{1,0:T(8,128)(2,1)} %all-gather.2.cloned.1.call-done, s32[1024]{0:T(1024)S(1)} %pad_clamp_fusion), kind=kCustom, calls=%fused_computation | custom fusion | bytes 525312 | tf_op jit(solution)/shard_map/gather | solution.py:78
  101.1 0.2 convert_reduce_fusion
  101.3 0.2 fusion.38
  101.5 2.8 fusion.76
  104.3 0.8 slice_bitcast_fusion
  105.1 0.1 copy.40
  105.3 0.1 copy.41
  105.4 1.6 divide_convert_fusion
  107.0 0.3 fusion.78
  107.4 0.1 fusion.40
  107.5 0.3 copy-done.2
  107.8 0.2 copy.35
  108.0 1.7 multiply_reduce_fusion.1
  109.7 2.1 fusion.75
  111.8 0.1 broadcast_add_fusion
  111.9 0.1 copy.36
  112.1 2.0 fusion.26
  114.1 0.2 fusion.80
  114.4 1.0 fusion.79
  115.4 0.9 fusion.81
  116.3 0.1 copy.37
  116.5 1.8 copy.38
  118.3 1.8 copy.39
  120.1 3.4 multiply_reduce_fusion
  123.4 1.0 fusion.74
  124.5 2.9 scatter_custom_fusion.1
  127.4 4.2 all-to-all-start.1
  131.6 0.2 all-reduce.6.cloned.1.call-start
  131.9 0.5 broadcast.379
  132.4 0.7 reduce.15
  133.0 0.1 reshape.502
  133.1 14.6 %all-to-all-done.1 = bf16[16,32,512]{2,1,0:T(8,128)(2,1)} async-done(((bf16[16,32,512]{2,1,0:T(8,128)(2,1)}), bf16[16,32,512]{2,1,0:T(8,128)(2,1)}, u32[]{:S(2)}, u32[]{:S(2)}) %all-to-all-start.1) | async-done | bytes 524320 | tf_op jit(solution)/shard_map/all_to_all | solution.py:94
  147.7 5.3 scatter_custom_fusion.2
  153.0 2.4 collective-permute-start
  155.5 36.2 %collective-permute-done = f32[768,512]{1,0:T(8,128)S(1)} collective-permute-done((f32[768,512]{1,0:T(8,128)}, f32[768,512]{1,0:T(8,128)S(1)}, u32[]{:S(2)}, u32[]{:S(2)}) %collective-permute-start) | collective-permute-done | bytes 1572896 | tf_op jit(solution)/shard_map/ppermute | solution.py:111
  191.7 1.8 add.132
  193.4 2.4 collective-permute-start.1
  195.8 70.9 %collective-permute-done.1 = f32[768,512]{1,0:T(8,128)S(1)} collective-permute-done((f32[768,512]{1,0:T(8,128)S(1)}, f32[768,512]{1,0:T(8,128)S(1)}, u32[]{:S(2)}, u32[]{:S(2)}) %collective-permute-start.1) | collective-permute-done | bytes 1572896 | tf_op jit(solution)/shard_map/ppermute | solution.py:111
  266.8 0.3 add.133
  267.1 4.7 collective-permute-start.2
  271.8 70.3 %collective-permute-done.2 = f32[768,512]{1,0:T(8,128)S(1)} collective-permute-done((f32[768,512]{1,0:T(8,128)S(1)}, f32[768,512]{1,0:T(8,128)S(1)}, u32[]{:S(2)}, u32[]{:S(2)}) %collective-permute-start.2) | collective-permute-done | bytes 1572896 | tf_op jit(solution)/shard_map/ppermute | solution.py:111
  342.1 0.3 add.134
  342.5 3.4 collective-permute-start.3
  345.8 34.9 %collective-permute-done.3 = f32[768,512]{1,0:T(8,128)S(1)} collective-permute-done((f32[768,512]{1,0:T(8,128)S(1)}, f32[768,512]{1,0:T(8,128)S(1)}, u32[]{:S(2)}, u32[]{:S(2)}) %collective-permute-start.3) | collective-permute-done | bytes 1572896 | tf_op jit(solution)/shard_map/ppermute | solution.py:111
  380.7 1.5 add.135
  382.2 4.9 collective-permute-start.4
  387.1 2.5 fusion.45
  389.5 0.0 all-reduce.6.cloned.1.call-update
  389.6 269.0 %all-reduce.6.cloned.1.call-done = f32[512,512]{1,0:T(8,128)} async-done(((f32[512,512]{1,0:T(8,128)}), f32[512,512]{1,0:T(8,128)}) %all-reduce.6.cloned.1.call-update) | async-done | bytes 1048592 | tf_op jit(solution)/shard_map/psum | solution.py:115
  658.6 2.1 multiply_convert_fusion
  660.7 3.4 add.136
  (31 shorter events, 0.2 us)
Async XLA Ops:
  7.2 94.4 %copy-start = (bf16[512,2048]{1,0:T(8,128)(2,1)S(1)}, bf16[512,2048]{1,0:T(8,128)(2,1)}, u32[]{:S(2)}) copy-start(bf16[512,2048]{1,0:T(8,128)(2,1)} %param.11) | copy-start | bytes 6291460
  7.2 86.5 %all-gather.2.cloned.1.call-start = ((), (), s32[]{:S(2)}) async-start(), calls=%async_computation.2 | async-start | bytes 13369344 | tf_op jit(solution)/shard_map/all_gather | solution.py:76
  13.1 114.3 %all-to-all-start = ((s32[16,1,32]{2,1,0:T(1,128)}), s32[16,1,32]{2,1,0:T(1,128)S(1)}, u32[]{:S(2)}, u32[]{:S(2)}) async-start(s32[16,1,32]{2,1,0:T(1,128)} %all_to_all.9), calls=%async_computation | async-start | bytes 16384 | tf_op jit(solution)/shard_map/all_to_all | solution.py:72
  105.2 1.8 copy-start.4
  105.4 1.6 copy-start.6
  105.4 1.6 copy-start.8
  107.0 0.8 copy-start.2
  112.0 2.1 copy-start.5
  112.1 2.3 copy-start.7
  114.1 1.3 copy-start.3
  120.1 4.4 copy-start.1
  127.4 20.3 %all-to-all-start.1 = ((bf16[16,32,512]{2,1,0:T(8,128)(2,1)}), bf16[16,32,512]{2,1,0:T(8,128)(2,1)}, u32[]{:S(2)}, u32[]{:S(2)}) async-start(bf16[16,32,512]{2,1,0:T(8,128)(2,1)} %bitcast.120), calls=%async_computation.1 | async-start | bytes 1048576 | tf_op jit(solution)/shard_map/all_to_all | solution.py:94
  131.6 526.9 %all-reduce.6.cloned.1.call-start = ((), (), s32[]{:S(2)}) async-start(), calls=%async_computation.3 | async-start | bytes 2097152 | tf_op jit(solution)/shard_map/psum | solution.py:115
  153.0 38.6 %collective-permute-start = (f32[768,512]{1,0:T(8,128)}, f32[768,512]{1,0:T(8,128)S(1)}, u32[]{:S(2)}, u32[]{:S(2)}) collective-permute-start(f32[768,512]{1,0:T(8,128)} %scatter_custom_fusion.2), channel_id=1, source_target_pairs={{0,16},{16,0},{32,48},{48,32},{64,80},{80,64},{96,112},{112,96},{1... | collective-permute-start | bytes 4718600 | tf_op jit(solution)/shard_map/ppermute | solution.py:111
  193.4 73.3 %collective-permute-start.1 = (f32[768,512]{1,0:T(8,128)S(1)}, f32[768,512]{1,0:T(8,128)S(1)}, u32[]{:S(2)}, u32[]{:S(2)}) collective-permute-start(f32[768,512]{1,0:T(8,128)S(1)} %add.132), channel_id=1, source_target_pairs={{0,32},{16,48},{32,0},{48,16},{64,96},{80,112},{96,64},{112,80},{1... | collective-permute-start | bytes 4718600 | tf_op jit(solution)/shard_map/ppermute | solution.py:111
  267.1 75.0 %collective-permute-start.2 = (f32[768,512]{1,0:T(8,128)S(1)}, f32[768,512]{1,0:T(8,128)S(1)}, u32[]{:S(2)}, u32[]{:S(2)}) collective-permute-start(f32[768,512]{1,0:T(8,128)S(1)} %add.133), channel_id=1, source_target_pairs={{0,64},{16,80},{32,96},{48,112},{64,0},{80,16},{96,32},{112,48},{1... | collective-permute-start | bytes 4718600 | tf_op jit(solution)/shard_map/ppermute | solution.py:111
  342.5 38.2 %collective-permute-start.3 = (f32[768,512]{1,0:T(8,128)S(1)}, f32[768,512]{1,0:T(8,128)S(1)}, u32[]{:S(2)}, u32[]{:S(2)}) collective-permute-start(f32[768,512]{1,0:T(8,128)S(1)} %add.134), channel_id=1, source_target_pairs={{0,128},{16,144},{32,160},{48,176},{64,192},{80,208},{96,224},{112... | collective-permute-start | bytes 4718600 | tf_op jit(solution)/shard_map/ppermute | solution.py:111
  382.2 278.5 %collective-permute-start.4 = (f32[768,512]{1,0:T(8,128)}, f32[768,512]{1,0:T(8,128)}, u32[]{:S(2)}, u32[]{:S(2)}) collective-permute-start(f32[768,512]{1,0:T(8,128)} %add.135), channel_id=1, source_target_pairs={{0,256},{16,272},{32,288},{48,304},{64,320},{80,336},{96,352},{112... | collective-permute-start | bytes 4718600 | tf_op jit(solution)/shard_map/ppermute | solution.py:111
Sparse Core Ops, SparseCore 0:
  10.1 83.4 all-gather.1
  389.7 268.8 all-reduce.5
